TPU v7x, 32 devices: a whole 2x2x4 slice. The times are simulated.
32 devices in a mesh: bins: 8 (over y, x, core), shells: 4 (over z).
Axes of the slice: x: 2, y: 2, z: 4, core: 2. Of those that a mesh axis runs over, the one named last changes fastest.
Arguments:
- map_tiles: bfloat16 [4, 4, 64, 8192], P('shells', None, None, 'bins'), may hold values from -3 to 3
- images: bfloat16 [2048, 4, 2, 8192], P('bins', 'shells'), may hold values from -6 to 6
- pose_bin: int32 [2048, 1], P('bins'), may hold values from 0 to 7; in each aligned block of 256 rows (0 to 255, 256 to 511, ...) at most 64 rows name the same one
- rot_index: int32 [2048], P('bins'), may hold values from 0 to 63
- shift_index: int32 [2048], P('bins'), may hold values from 0 to 48
- defocus_class: int32 [2048], P('bins'), may hold values from 0 to 15
- tile_slots: int32 [8, 4, 2], replicated, may hold values from -1 to 3, as said below
Outputs:
- map_gradient: float32 [4, 4, 64, 8192], P(None, None, 'shells', 'bins')
- particle_loss: float32 [2048, 4], P('bins', 'shells')
Inputs may be any that keep to these rules, and one draw needn't show every extreme that they name: `pose_bin`: among the 256 particles of one device of bins, at most 64 share a pose bin, a bound that some block reaches of them. `tile_slots`: the tiles listed for one bin and band are distinct, slot 0 always holds a tile, and -1 is only followed by -1; some bin has all 2 slots filled in every band.
All inputs are finite; a program needn't handle non-finite values.
Results may differ from a plain program's by a relative error of at most 0.00081.
Values may be sent and summed in bfloat16 or wider, within the bound.
A program may use at most 256 MiB of HBM per device.

v0:
```python
import math

import jax
import jax.numpy as jnp
from jax import lax
from jax.sharding import PartitionSpec as P

ROTS = 64
DEFOCI = 16


NOISE_PRECISION = 4.0
AMPLITUDE = 0.07


def plane_weights(rotation, bin_value, tile_safe, band_value, plane_count):
    pose_angle = (
        2.0 * math.pi / ROTS * rotation.astype(jnp.float32)
        + 0.7 * bin_value.astype(jnp.float32)
        + 1.3 * tile_safe.astype(jnp.float32)
        + 0.5 * band_value
    )
    centre = 0.5 * (plane_count - 1) + 0.45 * plane_count * jnp.sin(pose_angle)
    offset = (jnp.arange(plane_count, dtype=jnp.float32) - centre[..., None]) / 1.5
    return jnp.exp(-0.5 * offset * offset).astype(jnp.bfloat16)


def pixel_terms(tile_safe, shifts, defocus, band_value, plane_count, band_count):
    cell_index = jnp.arange(plane_count * plane_count, dtype=jnp.int32)
    cell_row = cell_index // plane_count
    cell_col = cell_index % plane_count
    freq_x = (plane_count * (tile_safe % 2) - plane_count)[..., None] + cell_row
    freq_y = (plane_count * (tile_safe // 2 % 2) - plane_count)[..., None] + cell_col
    real_x = freq_x.astype(jnp.float32)
    real_y = freq_y.astype(jnp.float32)
    radial = (real_x * real_x + real_y * real_y) / (2.0 * plane_count) ** 2 + (
        (band_value + 1.0) / band_count
    ) ** 2 / 4.0
    strength = 2.0 + 6.0 * defocus.astype(jnp.float32) / DEFOCI
    aberration = 8.0 * math.pi * strength[:, None, None] * radial
    contrast = -(
        math.sqrt(1.0 - AMPLITUDE * AMPLITUDE) * jnp.sin(aberration)
        + AMPLITUDE * jnp.cos(aberration)
    )
    shift_x = (shifts % 7 - 3).astype(jnp.float32)[:, None, None]
    shift_y = (shifts // 7 - 3).astype(jnp.float32)[:, None, None]
    phase_angle = 2.0 * math.pi / (4.0 * plane_count) * (real_x * shift_x + real_y * shift_y)
    return (contrast, jnp.cos(phase_angle), jnp.sin(phase_angle))


def band_terms(slices, observed, occupied, contrast, cosine, sine_part, grad_scale):
    pixel_count = slices.shape[-1] // 2
    slot_count = slices.shape[1]
    real_slice = slices[..., :pixel_count]
    imag_slice = slices[..., pixel_count:]
    measured = observed.astype(jnp.float32)
    model_real = contrast * (cosine * real_slice + sine_part * imag_slice)
    model_imag = contrast * (cosine * imag_slice - sine_part * real_slice)
    resid_real = occupied[..., None] * (model_real - measured[..., :pixel_count])
    resid_imag = occupied[..., None] * (model_imag - measured[..., pixel_count:])
    band_loss = (
        2.0
        * jnp.sum(resid_real * resid_real + resid_imag * resid_imag, axis=(1, 2))
        / (slot_count * 2 * pixel_count)
    )
    grad_real = grad_scale * contrast * (cosine * resid_real - sine_part * resid_imag)
    grad_imag = grad_scale * contrast * (sine_part * resid_real + cosine * resid_imag)
    return (band_loss, jnp.concatenate([grad_real, grad_imag], axis=-1).astype(jnp.bfloat16))


def stack_weights(weights, tile_safe, tile_count):
    selector = (tile_safe[..., None] == jnp.arange(tile_count, dtype=jnp.int32)).astype(
        jnp.bfloat16
    )
    stacked = selector[..., None] * weights[..., None, :]
    return stacked.reshape(weights.shape[0] * weights.shape[1], tile_count * weights.shape[2])


def contract_rows(stacked, slice_grad):
    return lax.dot_general(
        stacked, slice_grad, (((0,), (0,)), ((), ())), preferred_element_type=jnp.float32
    )


def on_device(map_tiles, images, pose_bin, rot_index, shift_index, defocus_class, tile_slots):
    band_index = lax.axis_index("shells")
    band_value = band_index.astype(jnp.float32)
    bin_count = lax.axis_size("bins")
    band_count = lax.axis_size("shells")
    part_count = images.shape[0]
    slot_count = images.shape[2]
    column_count = images.shape[3]
    tile_count = map_tiles.shape[1]
    plane_count = map_tiles.shape[2]
    shard_cols = map_tiles.shape[3]
    grad_scale = NOISE_PRECISION / math.sqrt(part_count * bin_count)
    band_slots = lax.dynamic_index_in_dim(tile_slots, band_index, 1, keepdims=False)
    map_shard = map_tiles[0].reshape(tile_count * plane_count, shard_cols)
    home_bins = pose_bin[:, 0]
    observed = images[:, 0]
    bin_match = (home_bins[:, None] == jnp.arange(bin_count, dtype=jnp.int32)[None, :]).astype(
        jnp.int32
    )
    capacity = 2 * part_count // bin_count
    earlier = jnp.cumsum(bin_match, axis=0) - bin_match
    slot_rank = jnp.sum(earlier * bin_match, axis=1)
    flat_slot = home_bins * capacity + slot_rank
    buffer_rows = bin_count * capacity
    send_images = (
        jnp.zeros((buffer_rows, slot_count, column_count), jnp.bfloat16).at[flat_slot].set(observed)
    )
    labels = jnp.stack([rot_index, shift_index, defocus_class, jnp.ones_like(rot_index)], axis=1)
    send_labels = jnp.zeros((buffer_rows, 4), jnp.int32).at[flat_slot].set(labels)
    got_images, got_labels = (
        lax.all_to_all(
            send_images.reshape(bin_count, capacity, slot_count, column_count),
            "bins",
            split_axis=0,
            concat_axis=0,
            tiled=True,
        ),
        lax.all_to_all(
            send_labels.reshape(bin_count, capacity, 4),
            "bins",
            split_axis=0,
            concat_axis=0,
            tiled=True,
        ),
    )
    routed = got_images.reshape(buffer_rows, slot_count, column_count)
    routed_labels = got_labels.reshape(buffer_rows, 4)
    own_bin = lax.axis_index("bins")
    own_tiles = lax.dynamic_index_in_dim(band_slots, own_bin, 0, keepdims=True)
    tile_safe = jnp.broadcast_to(jnp.maximum(own_tiles, 0), (buffer_rows, slot_count))
    occupied = (own_tiles >= 0).astype(jnp.float32) * routed_labels[:, 3:4].astype(jnp.float32)
    weights = plane_weights(routed_labels[:, 0:1], own_bin, tile_safe, band_value, plane_count)
    contrast, cosine, sine_part = pixel_terms(
        tile_safe, routed_labels[:, 1], routed_labels[:, 2], band_value, plane_count, band_count
    )
    stacked = stack_weights(weights, tile_safe, tile_count)
    slices = jnp.dot(
        stacked,
        lax.all_gather(map_shard, "bins", axis=1, tiled=True),
        preferred_element_type=jnp.float32,
    )
    band_loss, slice_grad = band_terms(
        slices.reshape(buffer_rows, slot_count, column_count),
        routed,
        occupied,
        contrast,
        cosine,
        sine_part,
        grad_scale,
    )
    local_grad = contract_rows(stacked, slice_grad.reshape(buffer_rows * slot_count, column_count))
    grad_shard = lax.psum_scatter(local_grad, "bins", scatter_dimension=1, tiled=True)
    loss_back = lax.all_to_all(
        band_loss.reshape(bin_count, capacity), "bins", split_axis=0, concat_axis=0, tiled=True
    )
    particle_loss = loss_back.reshape(buffer_rows)[flat_slot]
    gradient = lax.all_to_all(
        grad_shard.reshape(1, tile_count, plane_count, shard_cols),
        "shells",
        split_axis=2,
        concat_axis=0,
        tiled=True,
    )
    return (gradient, particle_loss[:, None])


def solution(mesh):
    return jax.shard_map(
        on_device,
        mesh=mesh,
        in_specs=(
            P("shells", None, None, "bins"),
            P("bins", "shells", None, None),
            P("bins", None),
            P("bins"),
            P("bins"),
            P("bins"),
            P(),
        ),
        out_specs=(P(None, None, "shells", "bins"), P("bins", "shells")),
        check_vma=False,
    )
```

profile of v0, /device:TPU:0, one launch (start us, length us, event | category | flops | bytes accessed | tf_op | source)
XLA Modules:
  0.0 821.0 jit_solution(8027164914713283549)
XLA Ops:
  7.2 0.7 fusion.22
  8.7 0.8 fusion.21
  9.4 0.7 compare_select_fusion.2
  10.2 0.8 add_add_fusion
  11.1 1.2 scatter_custom_fusion
  12.5 0.7 reshape.368
  13.2 5.2 all-to-all-start
  18.4 14.1 %broadcast_in_dim.52 = bf16[512,2,8192]{2,1,0:T(2,128)(2,1)} broadcast(bf16[]{:T(256)} %constant.185.clone.1), dimensions={} | broadcast | bytes 16777218 | tf_op jit(solution)/shard_map/broadcast_in_dim | solution.py:110
  32.5 64.6 %scatter_fusion = bf16[512,2,8192]{2,1,0:T(2,128)(2,1)} fusion(bf16[512,2,8192]{2,1,0:T(2,128)(2,1)} %broadcast_in_dim.52, s32[256]{0:T(256)S(1)} %bitcast.56, bf16[256,2,8192]{2,1,0:T(2,128)(2,1)} %bitcast.45), kind=kCustom, calls=%fused_computation.2 | custom fusion | bytes 25166848 | tf_op jit(solution)/shard_map/scatter | solution.py:110
  97.0 18.5 %copy.39 = bf16[8,64,2,8192]{3,1,2,0:T(8,128)(2,1)} copy(bf16[8,64,2,8192]{3,2,1,0:T(2,128)(2,1)} %bitcast.44) | data formatting | bytes 33554432 | tf_op jit(solution)/shard_map/reshape | solution.py:116
  115.5 5.9 all-to-all-start.1
  121.5 0.7 all-gather.2.cloned.1.call-update
  124.4 0.7 copy.37
  126.0 119.2 %all-gather.2.cloned.1.call-done = bf16[256,8192]{1,0:T(8,128)(2,1)} async-done(((bf16[256,1024]{1,0:T(8,128)(2,1)}), bf16[256,8192]{1,0:T(8,128)(2,1)}) %all-gather.2.cloned.1.call-update) | async-done | bytes 4194320 | tf_op jit(solution)/shard_map/all_gather | solution.py:143
  245.2 15.3 %fusion.8 = f32[512,2,8192]{2,0,1:T(8,128)} fusion(bf16[512,2,256]{0,2,1:T(8,128)(2,1)S(1)} %bitcast.46, bf16[256,8192]{1,0:T(8,128)(2,1)} %all-gather.2.cloned.1.call-done), kind=kOutput, calls=%fused_computation.18 | convolution fusion | flops 4294967296 | bytes 38273024 | tf_op jit(solution)/shard_map/dot_general | solution.py:141
  260.5 61.7 %all-to-all-done.1 = bf16[8,64,2,8192]{3,1,2,0:T(8,128)(2,1)} async-done(((bf16[8,64,2,8192]{3,1,2,0:T(8,128)(2,1)}), bf16[8,64,2,8192]{3,1,2,0:T(8,128)(2,1)}, u32[]{:S(2)}, u32[]{:S(2)}) %all-to-all-start.1) | async-done | bytes 16777248 | tf_op jit(solution)/shard_map/all_to_all | solution.py:115
  322.2 18.5 %copy.40 = f32[8,64,2,8192]{3,1,0,2:T(8,128)} copy(bf16[8,64,2,8192]{3,1,2,0:T(8,128)(2,1)} %all-to-all-done.1) | data formatting | bytes 50331648 | tf_op jit(solution)/shard_map/convert_element_type | solution.py:56
  340.7 153.8 %add_reduce_fusion = (f32[512]{0:T(512)S(1)}, f32[512,2,4096]{2,0,1:T(8,128)}, f32[512,2,4096]{2,0,1:T(8,128)}) fusion(f32[512,2,8192]{2,0,1:T(8,128)} %bitcast.43, f32[512,2,8192]{2,0,1:T(8,128)} %fusion.8, f32[512]{0:T(512)S(1)} %get-tuple-element.21, f32[512]{0:T(512)S(1)} %get-tuple-element.20, f32[]{:T(128)S(6)} %div.67, ...), kind=kLoop, calls=%fused_computation.11 | loop fusion | flops 142605824 | bytes 100716544 | tf_op jit(solution)/shard_map/reduce_sum | solution.py:63
  494.5 135.6 %multiply_convert_fusion.1 = (bf16[512,2,4096]{2,0,1:T(8,128)(2,1)}, bf16[512,2,4096]{2,0,1:T(8,128)(2,1)S(1)}) fusion(f32[512,2,4096]{2,0,1:T(8,128)} %get-tuple-element.12, f32[512,2,4096]{2,0,1:T(8,128)} %get-tuple-element.11, f32[512]{0:T(512)S(1)} %get-tuple-element.21, f32[512]{0:T(512)S(1)} %get-tuple-element.20, s32[4096]{0:T(1024)S(1)} %get-tuple-element.30, ...), kind=kLoop, calls=%fused_computation.13 | loop fusion | flops 121634816 | bytes 50378756 | tf_op jit(solution)/shard_map/convert.5
  630.1 22.3 %copy.42 = bf16[512,2,4096]{2,1,0:T(2,128)(2,1)} copy(bf16[512,2,4096]{2,0,1:T(8,128)(2,1)S(1)} %get-tuple-element.14) | data formatting | bytes 16777216 | tf_op jit(solution)/shard_map/convert.4
  652.5 13.1 %concatenate.10 = bf16[1024,4096]{1,0:T(8,128)(2,1)} reshape(bf16[512,2,4096]{2,1,0:T(2,128)(2,1)} %copy.42) | data formatting | bytes 16777216 | tf_op jit(solution)/shard_map/concatenate | solution.py:68
  665.6 16.4 %copy.41 = bf16[512,2,4096]{2,1,0:T(2,128)(2,1)} copy(bf16[512,2,4096]{2,0,1:T(8,128)(2,1)} %get-tuple-element.13) | data formatting | bytes 16777216 | tf_op jit(solution)/shard_map/convert.5
  682.0 13.1 %concatenate.9 = bf16[1024,4096]{1,0:T(8,128)(2,1)} reshape(bf16[512,2,4096]{2,1,0:T(2,128)(2,1)} %copy.41) | data formatting | bytes 16777216 | tf_op jit(solution)/shard_map/concatenate | solution.py:68
  695.0 13.2 %fusion.2 = f32[256,8192]{1,0:T(8,128)} fusion(bf16[1024,256]{1,0:T(8,128)(2,1)S(1)} %mul.246, bf16[1024,4096]{1,0:T(8,128)(2,1)} %concatenate.10, bf16[1024,4096]{1,0:T(8,128)(2,1)} %concatenate.9), kind=kOutput, calls=%fused_computation.7 | convolution fusion | flops 4328521728 | bytes 25690112 | tf_op jit(solution)/shard_map/dot_general | solution.py:80
  708.3 0.7 div.72
  708.9 3.3 all-to-all-start.3
  712.3 66.9 %reduce-scatter.2.cloned.1.call-done = f32[256,1024]{1,0:T(8,128)} async-done(((f32[256,8192]{1,0:T(8,128)}), f32[256,1024]{1,0:T(8,128)}) %reduce-scatter.2.cloned.1.call-update) | async-done | bytes 1048592 | tf_op jit(solution)/shard_map/reduce_scatter | solution.py:156
  779.2 2.9 copy.43
  782.1 4.6 all-to-all-start.2
  787.9 2.5 gather_fusion
  790.4 21.8 %all-to-all-done.2 = f32[1,4,64,1024]{3,1,0,2:T(4,128)S(1)} async-done(((f32[1,4,64,1024]{3,1,0,2:T(4,128)}), f32[1,4,64,1024]{3,1,0,2:T(4,128)S(1)}, u32[]{:S(2)}, u32[]{:S(2)}) %all-to-all-start.2) | async-done | bytes 1048608 | tf_op jit(solution)/shard_map/all_to_all | solution.py:161
  812.8 1.1 copy.45
  (42 shorter events, 6.1 us)
Async XLA Ops:
  13.2 102.4 %all-to-all-start = ((s32[8,1,256]{2,1,0:T(1,128)}), s32[8,1,256]{2,1,0:T(1,128)S(1)}, u32[]{:S(2)}, u32[]{:S(2)}) async-start(s32[8,1,256]{2,1,0:T(1,128)} %reshape.368), calls=%async_computation | async-start | bytes 16384 | tf_op jit(solution)/shard_map/all_to_all | solution.py:122
  115.5 6.7 copy-start
  115.5 206.6 %all-to-all-start.1 = ((bf16[8,64,2,8192]{3,1,2,0:T(8,128)(2,1)}), bf16[8,64,2,8192]{3,1,2,0:T(8,128)(2,1)}, u32[]{:S(2)}, u32[]{:S(2)}) async-start(bf16[8,64,2,8192]{3,1,2,0:T(8,128)(2,1)} %copy.39), calls=%async_computation.1 | async-start | bytes 33554432 | tf_op jit(solution)/shard_map/all_to_all | solution.py:115
  121.4 123.8 %all-gather.2.cloned.1.call-start = ((), (), s32[]{:S(2)}) async-start(), calls=%async_computation.5 | async-start | bytes 4718592 | tf_op jit(solution)/shard_map/all_gather | solution.py:143
  122.2 657.1 %reduce-scatter.2.cloned.1.call-start = ((), (), s32[]{:S(2)}) async-start(), calls=%async_computation.6 | async-start | bytes 9437184 | tf_op jit(solution)/shard_map/reduce_scatter | solution.py:156
  708.9 73.1 %all-to-all-start.3 = ((f32[8,1,64]{2,1,0:T(1,128)}), f32[8,1,64]{2,1,0:T(1,128)S(1)}, u32[]{:S(2)}, u32[]{:S(2)}) async-start(f32[8,1,64]{2,1,0:T(1,128)} %div.72), calls=%async_computation.4 | async-start | bytes 8192 | tf_op jit(solution)/shard_map/all_to_all | solution.py:157
  782.1 30.1 %all-to-all-start.2 = ((f32[1,4,64,1024]{3,1,0,2:T(4,128)}), f32[1,4,64,1024]{3,1,0,2:T(4,128)S(1)}, u32[]{:S(2)}, u32[]{:S(2)}) async-start(f32[1,4,64,1024]{3,1,0,2:T(4,128)} %copy.43), calls=%async_computation.3 | async-start | bytes 2097152 | tf_op jit(solution)/shard_map/all_to_all | solution.py:161
Sparse Core Ops, SparseCore 0:
  124.1 121.0 all-gather.1
  708.4 70.7 reduce-scatter.1
where the time goes:
time: 831 us; the launch traced here: 821 us
  other arithmetic  295 us (35%)
  waiting for transfers between devices  270 us (32%)
  local copies, waits for them, and re-layouts  193 us (23%)
  matrix products  28.5 us (3%)
  starting transfers between devices  19 us (2%)
  between operations  14.4 us (2%)
    reduce_sum x1, other arithmetic, band_terms(): jnp.sum(resid_real * resid_real + resid_imag * resid_imag, axis=(1, 2))  154 us
    another operation x3, other arithmetic  136 us
    all_gather x1, waiting for transfers between devices, on_device(): lax.all_gather(map_shard, 'bins', axis=1, tiled=True)  119 us
    reduce_scatter x1, waiting for transfers between devices, on_device(): lax.psum_scatter(local_grad, 'bins', scatter_dimension=1, tiled=True)  66.9 us
    scatter x1, local copies, waits for them, and re-layouts, on_device(): jnp.zeros((buffer_rows, slot_count, column_count), jnp.bfloat16)  64.6 us
    all_to_all x1, waiting for transfers between devices, on_device(): lax.all_to_all(send_images.reshape(bin_count, capacity, slot_count, colum...  61.7 us
    another operation x3, local copies, waits for them, and re-layouts  38.7 us
    concatenate x2, local copies, waits for them, and re-layouts, band_terms(): jnp.concatenate([grad_real, grad_imag], axis=-1).astype(jnp.bfloat16)  26.2 us
  transfers between devices with their start and end apart: 6, of which 4 were waited for; matrix products, arithmetic and copies ran while one was open for 15% of the time, Pallas kernels for 0%

commit v1 on v0

v1 whole, which is shorter than its diff:
```python
import math

import jax
import jax.numpy as jnp
from jax import lax
from jax.experimental import pallas as pl
from jax.experimental.pallas import tpu as pltpu
from jax.sharding import PartitionSpec as P

ROTS = 64
DEFOCI = 16
GRID = 7
NOISE_PRECISION = 4.0
AMPLITUDE = 0.07


def split_halves(table):
    rounded = lax.reduce_precision(table, 8, 7)
    high = rounded.astype(jnp.bfloat16)
    low = (table - rounded).astype(jnp.bfloat16)
    return jnp.concatenate([high, low], axis=0)


def contrast_table(band_value, plane_count, band_count):
    rows = jnp.arange(DEFOCI * 4, dtype=jnp.int32)[:, None]
    cell = jnp.arange(plane_count * plane_count, dtype=jnp.int32)[None, :]
    defocus = rows // 4
    real_x = (plane_count * (rows % 2) - plane_count + cell // plane_count).astype(jnp.float32)
    real_y = (plane_count * (rows // 2 % 2) - plane_count + cell % plane_count).astype(jnp.float32)
    radial = (real_x * real_x + real_y * real_y) / (2.0 * plane_count) ** 2 + (
        (band_value + 1.0) / band_count
    ) ** 2 / 4.0
    strength = 2.0 + 6.0 * defocus.astype(jnp.float32) / DEFOCI
    aberration = 8.0 * math.pi * strength * radial
    contrast = -(
        math.sqrt(1.0 - AMPLITUDE * AMPLITUDE) * jnp.sin(aberration)
        + AMPLITUDE * jnp.cos(aberration)
    )
    return split_halves(contrast)


def phase_table(plane_count, pad):
    rows = jnp.arange(GRID * GRID, dtype=jnp.int32)[:, None]
    cell = jnp.arange(plane_count * plane_count, dtype=jnp.int32)[None, :]
    turns = (cell // plane_count) * (rows % GRID - 3) + (cell % plane_count) * (rows // GRID - 3)
    angle = 2.0 * math.pi / (4.0 * plane_count) * turns.astype(jnp.float32)
    both = [split_halves(jnp.cos(angle)), split_halves(jnp.sin(angle))]
    used = 4 * GRID * GRID
    both.append(jnp.zeros((pad - used, cell.shape[1]), jnp.bfloat16))
    return jnp.concatenate(both, axis=0)


def selectors(shifts, defocus, tile_safe, pad):
    parity = tile_safe % 2 + 2 * (tile_safe // 2 % 2)
    pick = (
        (defocus * 4 + parity)[:, None]
        == (jnp.arange(2 * DEFOCI * 4, dtype=jnp.int32) % (DEFOCI * 4))[None, :]
    ).astype(jnp.bfloat16)
    sx = shifts % GRID - 3
    sy = shifts // GRID - 3
    quarter = ((1 - tile_safe % 2) * sx + (1 - tile_safe // 2 % 2) * sy + 64) % 4
    real_turn = jnp.where(quarter == 0, 1.0, jnp.where(quarter == 2, -1.0, 0.0))
    imag_turn = jnp.where(quarter == 1, -1.0, jnp.where(quarter == 3, 1.0, 0.0))
    column = jnp.arange(pad, dtype=jnp.int32)
    count = GRID * GRID
    match = (shifts[:, None] == (column % count)[None, :]).astype(jnp.float32)
    is_cos = (column < 2 * count).astype(jnp.float32)[None, :]
    is_sin = ((column >= 2 * count) & (column < 4 * count)).astype(jnp.float32)[None, :]
    cosine = match * (real_turn[:, None] * is_cos - imag_turn[:, None] * is_sin)
    sine = match * (imag_turn[:, None] * is_cos + real_turn[:, None] * is_sin)
    return pick, cosine.astype(jnp.bfloat16), sine.astype(jnp.bfloat16)


def row_weights(rotation, bins, tile_safe, occupied, band_value, tile_count, plane_count):
    pose_angle = (
        2.0 * math.pi / ROTS * rotation.astype(jnp.float32)
        + 0.7 * bins.astype(jnp.float32)
        + 1.3 * tile_safe.astype(jnp.float32)
        + 0.5 * band_value
    )
    centre = 0.5 * (plane_count - 1) + 0.45 * plane_count * jnp.sin(pose_angle)
    column = jnp.arange(tile_count * plane_count, dtype=jnp.int32)
    plane = (column % plane_count).astype(jnp.float32)
    offset = (plane[None, :] - centre[:, None]) / 1.5
    weights = jnp.exp(-0.5 * offset * offset)
    mine = (tile_safe[:, None] == (column // plane_count)[None, :]) & (occupied > 0)[:, None]
    return jnp.where(mine, weights, 0.0).astype(jnp.bfloat16)


def step_body(
    scale, w_ref, wt_ref, pick_ref, cos_ref, sin_ref, ctf_ref, phase_ref, map_ref, yr_ref, yi_ref,
    grad_ref, loss_ref,
):
    f32 = jnp.float32
    weights = w_ref[...]
    phases = phase_ref[...]
    part_a = jnp.dot(weights, map_ref[0, 0], preferred_element_type=f32)
    part_b = jnp.dot(weights, map_ref[1, 0], preferred_element_type=f32)
    contrast = jnp.dot(pick_ref[...], ctf_ref[...], preferred_element_type=f32)
    cosine = contrast * jnp.dot(cos_ref[...], phases, preferred_element_type=f32)
    sine = contrast * jnp.dot(sin_ref[...], phases, preferred_element_type=f32)
    resid_real = cosine * part_a + sine * part_b - yr_ref[...].astype(f32)
    resid_imag = cosine * part_b - sine * part_a - yi_ref[...].astype(f32)
    square = resid_real * resid_real + resid_imag * resid_imag
    total = square[:, :128]
    for at in range(128, square.shape[1], 128):
        total = total + square[:, at : at + 128]

    @pl.when(pl.program_id(0) == 0)
    def _():
        loss_ref[...] = jnp.zeros_like(loss_ref)

    loss_ref[...] += total
    cosine = scale * cosine
    sine = scale * sine
    grad_real = (cosine * resid_real - sine * resid_imag).astype(jnp.bfloat16)
    grad_imag = (sine * resid_real + cosine * resid_imag).astype(jnp.bfloat16)
    back = wt_ref[...]
    grad_ref[0, 0] = jnp.dot(back, grad_real, preferred_element_type=f32)
    grad_ref[1, 0] = jnp.dot(back, grad_imag, preferred_element_type=f32)


def local_step(scale, weights, pick, cosine, sine, ctf, phase, full_map, images):
    rows, depth = weights.shape
    halves, groups, _, cols = full_map.shape
    tile = min(256, cols)
    steps = groups * cols // tile
    per = cols // tile

    def whole(a):
        return pl.BlockSpec(a.shape, lambda g: (0,) * a.ndim)

    back = weights.T
    split = pl.BlockSpec((halves, 1, depth, tile), lambda g: (0, g // per, 0, g % per))
    return pl.pallas_call(
        lambda *refs: step_body(scale, *refs),
        grid=(steps,),
        in_specs=[
            whole(weights), whole(back), whole(pick), whole(cosine), whole(sine),
            pl.BlockSpec((ctf.shape[0], tile), lambda g: (0, g)),
            pl.BlockSpec((phase.shape[0], tile), lambda g: (0, g)),
            split,
            pl.BlockSpec((rows, tile), lambda g: (0, g)),
            pl.BlockSpec((rows, tile), lambda g: (0, steps + g)),
        ],
        out_specs=[split, pl.BlockSpec((rows, 128), lambda g: (0, 0))],
        out_shape=[
            jax.ShapeDtypeStruct(full_map.shape, jnp.float32),
            jax.ShapeDtypeStruct((rows, 128), jnp.float32),
        ],
        compiler_params=pltpu.CompilerParams(vmem_limit_bytes=48 * 2**20),
    )(weights, back, pick, cosine, sine, ctf, phase, full_map, images, images)


def on_device(map_tiles, images, pose_bin, rot_index, shift_index, defocus_class, tile_slots):
    band_index = lax.axis_index("shells")
    band_value = band_index.astype(jnp.float32)
    bin_count = lax.axis_size("bins")
    band_count = lax.axis_size("shells")
    part_count, _, slot_count, column_count = images.shape
    _, tile_count, plane_count, shard_cols = map_tiles.shape
    rows = part_count * slot_count
    depth = tile_count * plane_count
    grad_scale = NOISE_PRECISION / math.sqrt(part_count * bin_count)
    gathered = lax.all_gather(map_tiles.reshape(1, depth, shard_cols), "bins", axis=0, tiled=True)
    band_slots = lax.dynamic_index_in_dim(tile_slots, band_index, 1, keepdims=False)

    def per_row(values):
        return jnp.repeat(values, slot_count)

    bins = per_row(pose_bin[:, 0])
    slot = jnp.arange(rows, dtype=jnp.int32) % slot_count
    flat_slots = band_slots.reshape(-1)
    chosen = (bins * slot_count + slot)[:, None] == jnp.arange(flat_slots.shape[0])[None, :]
    tiles = jnp.sum(jnp.where(chosen, flat_slots[None, :], 0), axis=1)
    occupied = (tiles >= 0).astype(jnp.float32)
    tile_safe = jnp.maximum(tiles, 0)
    weights = row_weights(
        per_row(rot_index), bins, tile_safe, occupied, band_value, tile_count, plane_count
    )
    pad = 256
    pick, cosine, sine = selectors(per_row(shift_index), per_row(defocus_class), tile_safe, pad)
    ctf = contrast_table(band_value, plane_count, band_count)
    phase = phase_table(plane_count, pad)
    partial, losses = local_step(
        grad_scale, weights, pick, cosine, sine, ctf, phase,
        gathered.reshape(2, bin_count // 2, depth, shard_cols),
        images.reshape(rows, column_count),
    )
    band_loss = (
        2.0
        * jnp.sum((losses * occupied[:, None]).reshape(part_count, slot_count * 128), axis=1)
        / (slot_count * column_count)
    )
    grad_shard = lax.psum_scatter(
        partial.reshape(bin_count, depth, shard_cols), "bins", scatter_dimension=0, tiled=True
    )
    gradient = lax.all_to_all(
        grad_shard.reshape(1, tile_count, plane_count, shard_cols),
        "shells",
        split_axis=2,
        concat_axis=0,
        tiled=True,
    )
    return (gradient, band_loss[:, None])


def solution(mesh):
    return jax.shard_map(
        on_device,
        mesh=mesh,
        in_specs=(
            P("shells", None, None, "bins"),
            P("bins", "shells", None, None),
            P("bins", None),
            P("bins"),
            P("bins"),
            P("bins"),
            P(),
        ),
        out_specs=(P(None, None, "shells", "bins"), P("bins", "shells")),
        check_vma=False,
    )
```

time: 831 us -> 193 us (0.23)
  other arithmetic: 295 us -> 17.2 us
  waiting for transfers between devices: 270 us -> 99.5 us
  local copies, waits for them, and re-layouts: 193 us -> 34.8 us
  matrix products: 28.5 us -> 0 us
  Pallas kernels: 0 us -> 20.8 us
  starting transfers between devices: 19 us -> 4.67 us
    reduce_sum x2 -> x3, other arithmetic: 155 us -> 1.08 us  [the longest x1 0.74 us: on_device(): tiles = jnp.sum(jnp.where(chosen, flat_slots[None, :], 0), axis=1)]
    another operation x4 -> x0, other arithmetic: 137 us -> none
    all_gather x1, waiting for transfers between devices: 119 us -> 0.02 us  [on_device(): lax.all_gather(map_tiles.reshape(1, depth, shard_cols), 'bins', axis=0, t...]
    scatter x2 -> x0, local copies, waits for them, and re-layouts: 65.8 us -> none  [the longest x1 64.6 us: on_device(): jnp.zeros((buffer_rows, slot_count, column_count), jnp.bfloat16)]
    all_to_all x3 -> x0, waiting for transfers between devices: 61.7 us -> none  [the longest x1 61.7 us: on_device(): lax.all_to_all(send_images.reshape(bin_count, capacity, slot_count, colum...]
    another operation x5 -> x0, local copies, waits for them, and re-layouts: 38.9 us -> none
    dot_general x2 -> x0, matrix products: 28.5 us -> none  [the longest x1 15.3 us: on_device(): jnp.dot(stacked, lax.all_gather(map_shard, 'bins', axis=1, tiled=True), p...]
    pallas_call x0 -> x1, Pallas kernels: none -> 20.8 us  [local_step(): pl.pallas_call(lambda *refs: step_body(scale, *refs), grid=(steps,), in_s...]
  transfers between devices with their start and end apart: 6 -> 3, of which waited for: 4 -> 2; matrix products, arithmetic and copies ran while one was open for 15% -> 23% of each run, Pallas kernels for 0% -> 0%
where the time goes in v1:
time: 193 us; the launch traced here: 191 us
  waiting for transfers between devices  99.5 us (52%)
  local copies, waits for them, and re-layouts  34.8 us (18%)
  Pallas kernels  20.8 us (11%)
  other arithmetic  17.2 us (9%)
  between operations  14.3 us (7%)
  starting transfers between devices  4.67 us (2%)
    reduce_scatter x1, waiting for transfers between devices, on_device(): lax.psum_scatter(partial.reshape(bin_count, depth, shard_cols), 'bins', s...  74.3 us
    all_to_all x1, waiting for transfers between devices, on_device(): lax.all_to_all(grad_shard.reshape(1, tile_count, plane_count, shard_cols)...  24.5 us
    pallas_call x1, Pallas kernels, local_step(): pl.pallas_call(lambda *refs: step_body(scale, *refs), grid=(steps,), in_s...  20.8 us
    reshape x1, local copies, waits for them, and re-layouts, on_device(): images.reshape(rows, column_count)  13.2 us
    concatenate x1, local copies, waits for them, and re-layouts, phase_table(): return jnp.concatenate(both, axis=0)  10.3 us
    convert_element_type x1, other arithmetic, split_halves(): high = rounded.astype(jnp.bfloat16)  5.07 us
    convert_element_type x1, other arithmetic, split_halves(): low = (table - rounded).astype(jnp.bfloat16)  4.96 us
    unnamed x17, local copies, waits for them, and re-layouts  4.67 us
  transfers between devices with their start and end apart: 3, of which 2 were waited for; matrix products, arithmetic and copies ran while one was open for 23% of the time, Pallas kernels for 0%

profile of v1, /device:TPU:0, one launch (start us, length us, event | category | flops | bytes accessed | tf_op | source)
XLA Modules:
  0.0 191.3 jit_solution(9471078559381811411)
XLA Ops:
  7.2 0.7 all-gather.2.cloned.1.call-update
  8.1 0.6 broadcast_in_dim.71
  8.7 0.7 broadcast_multiply_fusion.2
  9.4 0.1 mul.319
  9.6 0.7 convert_multiply_fusion.1
  10.3 0.7 multiply_add_fusion.1
  11.1 0.1 add.397
  11.2 0.7 broadcast_multiply_fusion.1
  12.0 0.7 mul.337
  12.7 0.8 broadcast_in_dim.78
  13.6 13.2 %reshape.460.refs_8_.refs_9_ = bf16[512,8192]{1,0:T(8,128)(2,1)} reshape(bf16[256,1,2,8192]{3,2,1,0:T(2,128)(2,1)} %param.8) | data formatting | bytes 16777216 | tf_op jit(solution)/shard_map/reshape | solution.py:188
  26.9 5.0 %fusion.2 = (bf16[49,4096]{1,0:T(8,128)(2,1)S(1)}, bf16[49,4096]{1,0:T(8,128)(2,1)S(1)}, bf16[49,4096]{1,0:T(8,128)(2,1)}, bf16[49,4096]{1,0:T(8,128)(2,1)}) fusion(s32[49]{0:T(128)S(1)} %get-tuple-element.35, s32[4096]{0:T(1024)S(1)} %get-tuple-element.30, s32[49]{0:T(128)S(1)} %get-tuple-element.34, s32[4096]{0:T(1024)S(1)} %get-tuple-element.31), kind=kLoop, calls=%fused_computation.10 | loop fusion | flops 2609152 | bytes 1638792 | tf_op jit(solution)/shard_map/convert_element_type | solution.py:20
  31.9 10.3 %concatenate.7.refs_6_ = bf16[256,4096]{1,0:T(8,128)(2,1)S(1)} concatenate(bf16[49,4096]{1,0:T(8,128)(2,1)} %get-tuple-element.21, bf16[49,4096]{1,0:T(8,128)(2,1)} %get-tuple-element.20, bf16[49,4096]{1,0:T(8,128)(2,1)S(1)} %get-tuple-element.19, bf16[49,4096]{1,0:T(8,128)(2,1)S(1)} %get-tuple-element.18, bf16[60,4096]{1,0:T(8,128)(2,1)S(1)} %broadcast_in_dim.81), dimensions={0} | concatenate | bytes 4194304 | tf_op jit(solution)/shard_map/concatenate | solution.py:50
  42.4 0.7 select_reduce_fusion
  43.2 0.7 add_add_fusion
  44.0 0.3 fusion.14.refs_1_
  44.3 1.5 fusion.6
  45.8 5.1 %reduce-precision_convert_fusion = (bf16[64,4096]{1,0:T(8,128)(2,1)S(1)}, bf16[64,4096]{1,0:T(8,128)(2,1)S(1)}) fusion(f32[]{:T(128)S(6)} %div.127, s32[4096]{0:T(1024)} %copy-done.6, s32[64]{0:T(128)S(1)} %get-tuple-element.33, s32[4096]{0:T(1024)} %copy-done.7, s32[64]{0:T(128)S(1)} %get-tuple-element.32, f32[64]{0:T(128)S(1)} %fusion.40), kind=kLoop, calls=%fused_computation.1 | loop fusion | flops 4718592 | bytes 1082116 | tf_op jit(solution)/shard_map/convert_element_type | solution.py:19
  51.0 0.9 copy-done.1
  51.9 0.9 copy-done.2
  52.9 0.9 copy-done.3
  53.8 20.8 %shard_map.86 = (f32[2,4,256,1024]{3,2,1,0:T(8,128)}, f32[512,128]{1,0:T(8,128)S(1)}) custom-call(bf16[512,256]{1,0:T(8,128)(2,1)S(1)} %copy-done.3, bf16[256,512]{1,0:T(8,128)(2,1)S(1)} %fusion.14.refs_1_, bf16[512,128]{1,0:T(8,128)(2,1)S(1)} %compare_convert_fusion.refs_2_, bf16[512,256]{1,0:T(8,128)(2,1)S(1)} %copy-done.2, ...), custom_call_target="tpu_custom_call" | custom-call | tf_op jit(solution)/shard_map/pallas_call | solution.py:135
  74.7 0.7 copy-done.4
  75.4 74.3 %reduce-scatter.2.cloned.1.call-done = f32[1,256,1024]{2,1,0:T(8,128)} async-done(((f32[8,256,1024]{2,1,0:T(8,128)}), f32[1,256,1024]{2,1,0:T(8,128)}) %reduce-scatter.2.cloned.1.call-update) | async-done | bytes 1048592 | tf_op jit(solution)/shard_map/reduce_scatter | solution.py:195
  149.7 2.9 %copy.20 = f32[1,4,64,1024]{3,1,0,2:T(4,128)} copy(f32[1,4,64,1024]{3,2,1,0:T(8,128)} %bitcast.17) | data formatting | bytes 2097152 | tf_op jit(solution)/shard_map/reshape | solution.py:199
  152.6 4.6 %all-to-all-start = ((f32[1,4,64,1024]{3,1,0,2:T(4,128)}), f32[1,4,64,1024]{3,1,0,2:T(4,128)S(1)}, u32[]{:S(2)}, u32[]{:S(2)}) async-start(f32[1,4,64,1024]{3,1,0,2:T(4,128)} %copy.20), calls=%async_computation.1 | async-start | bytes 2097152 | tf_op jit(solution)/shard_map/all_to_all | solution.py:198
  157.2 0.2 multiply_reduce_fusion
  157.4 0.1 reduce_sum.27
  157.7 0.6 broadcast_multiply_fusion
  158.2 24.5 %all-to-all-done = f32[1,4,64,1024]{3,1,0,2:T(4,128)S(1)} async-done(((f32[1,4,64,1024]{3,1,0,2:T(4,128)}), f32[1,4,64,1024]{3,1,0,2:T(4,128)S(1)}, u32[]{:S(2)}, u32[]{:S(2)}) %all-to-all-start) | async-done | bytes 1048608 | tf_op jit(solution)/shard_map/all_to_all | solution.py:198
  182.7 0.6 copy.21
  183.4 1.1 copy.22
  (40 shorter events, 1.1 us)
Async XLA Ops:
  7.2 0.8 copy-start
  7.2 43.8 %all-gather.2.cloned.1.call-start = ((), (), s32[]{:S(2)}) async-start(), calls=%async_computation.2 | async-start | bytes 4718592 | tf_op jit(solution)/shard_map/all_gather | solution.py:165
  7.9 141.8 %reduce-scatter.2.cloned.1.call-start = ((), (), s32[]{:S(2)}) async-start(), calls=%async_computation.3 | async-start | bytes 9437184 | tf_op jit(solution)/shard_map/reduce_scatter | solution.py:195
  26.9 5.0 %copy-start.6 = (s32[4096]{0:T(1024)}, s32[4096]{0:T(1024)S(1)}, u32[]{:S(2)}) copy-start(s32[4096]{0:T(1024)S(1)} %get-tuple-element.30) | copy-start | bytes 49156
  26.9 5.0 %copy-start.7 = (s32[4096]{0:T(1024)}, s32[4096]{0:T(1024)S(1)}, u32[]{:S(2)}) copy-start(s32[4096]{0:T(1024)S(1)} %get-tuple-element.31) | copy-start | bytes 49156
  51.0 1.0 copy-start.1
  51.9 0.9 copy-start.2
  52.9 0.9 copy-start.3
  74.7 0.7 copy-start.4
  75.4 81.8 %copy-start.5 = (f32[512,128]{1,0:T(8,128)S(1)}, f32[512,128]{1,0:T(8,128)}, u32[]{:S(2)}) copy-start(f32[512,128]{1,0:T(8,128)} %copy-done.4) | copy-start | bytes 786436
  152.6 30.2 %all-to-all-start = ((f32[1,4,64,1024]{3,1,0,2:T(4,128)}), f32[1,4,64,1024]{3,1,0,2:T(4,128)S(1)}, u32[]{:S(2)}, u32[]{:S(2)}) async-start(f32[1,4,64,1024]{3,1,0,2:T(4,128)} %copy.20), calls=%async_computation.1 | async-start | bytes 2097152 | tf_op jit(solution)/shard_map/all_to_all | solution.py:198
Sparse Core Ops, SparseCore 0:
  9.9 39.3 all-gather.1
  75.5 74.1 reduce-scatter.1

commit v2 on v1

--- a/solution.py
+++ b/solution.py
@@ -40,13 +40,18 @@
 
 
 def phase_table(plane_count, pad):
-    rows = jnp.arange(GRID * GRID, dtype=jnp.int32)[:, None]
+    steps = (jnp.arange(8, dtype=jnp.int32) - 3)[:, None]
     cell = jnp.arange(plane_count * plane_count, dtype=jnp.int32)[None, :]
-    turns = (cell // plane_count) * (rows % GRID - 3) + (cell % plane_count) * (rows // GRID - 3)
-    angle = 2.0 * math.pi / (4.0 * plane_count) * turns.astype(jnp.float32)
-    both = [split_halves(jnp.cos(angle)), split_halves(jnp.sin(angle))]
-    used = 4 * GRID * GRID
-    both.append(jnp.zeros((pad - used, cell.shape[1]), jnp.bfloat16))
+    unit = 2.0 * math.pi / (4.0 * plane_count)
+    along_x = unit * ((cell // plane_count) * steps).astype(jnp.float32)
+    along_y = unit * ((cell % plane_count) * steps).astype(jnp.float32)
+    cos_x, sin_x, cos_y, sin_y = lax.optimization_barrier(
+        (jnp.cos(along_x), jnp.sin(along_x), jnp.cos(along_y[:GRID]), jnp.sin(along_y[:GRID]))
+    )
+    cosine = cos_y[:, None] * cos_x[None] - sin_y[:, None] * sin_x[None]
+    sine = sin_y[:, None] * cos_x[None] + cos_y[:, None] * sin_x[None]
+    both = [split_halves(t.reshape(GRID * 8, cell.shape[1])) for t in (cosine, sine)]
+    both.append(jnp.zeros((pad - 4 * GRID * 8, cell.shape[1]), jnp.bfloat16))
     return jnp.concatenate(both, axis=0)
 
 
@@ -62,8 +67,8 @@
     real_turn = jnp.where(quarter == 0, 1.0, jnp.where(quarter == 2, -1.0, 0.0))
     imag_turn = jnp.where(quarter == 1, -1.0, jnp.where(quarter == 3, 1.0, 0.0))
     column = jnp.arange(pad, dtype=jnp.int32)
-    count = GRID * GRID
-    match = (shifts[:, None] == (column % count)[None, :]).astype(jnp.float32)
+    count = GRID * 8
+    match = ((shifts + shifts // GRID)[:, None] == (column % count)[None, :]).astype(jnp.float32)
     is_cos = (column < 2 * count).astype(jnp.float32)[None, :]
     is_sin = ((column >= 2 * count) & (column < 4 * count)).astype(jnp.float32)[None, :]
     cosine = match * (real_turn[:, None] * is_cos - imag_turn[:, None] * is_sin)
@@ -87,69 +92,157 @@
     return jnp.where(mine, weights, 0.0).astype(jnp.bfloat16)
 
 
-def step_body(
-    scale, w_ref, wt_ref, pick_ref, cos_ref, sin_ref, ctf_ref, phase_ref, map_ref, yr_ref, yi_ref,
-    grad_ref, loss_ref,
+def fused_step(
+    scale, bands, w_ref, wt_ref, pick_ref, cos_ref, sin_ref, ctf_ref, phase_ref, map_ref, img_ref,
+    out_ref, loss_ref,
+    mine, theirs, pair_in, chip_in, final,
+    pair_send, pair_recv, chip_send, chip_recv, band_send, band_recv,
 ):
     f32 = jnp.float32
-    weights = w_ref[...]
-    phases = phase_ref[...]
-    part_a = jnp.dot(weights, map_ref[0, 0], preferred_element_type=f32)
-    part_b = jnp.dot(weights, map_ref[1, 0], preferred_element_type=f32)
-    contrast = jnp.dot(pick_ref[...], ctf_ref[...], preferred_element_type=f32)
-    cosine = contrast * jnp.dot(cos_ref[...], phases, preferred_element_type=f32)
-    sine = contrast * jnp.dot(sin_ref[...], phases, preferred_element_type=f32)
-    resid_real = cosine * part_a + sine * part_b - yr_ref[...].astype(f32)
-    resid_imag = cosine * part_b - sine * part_a - yi_ref[...].astype(f32)
-    square = resid_real * resid_real + resid_imag * resid_imag
-    total = square[:, :128]
-    for at in range(128, square.shape[1], 128):
-        total = total + square[:, at : at + 128]
-
-    @pl.when(pl.program_id(0) == 0)
-    def _():
-        loss_ref[...] = jnp.zeros_like(loss_ref)
-
-    loss_ref[...] += total
-    cosine = scale * cosine
-    sine = scale * sine
-    grad_real = (cosine * resid_real - sine * resid_imag).astype(jnp.bfloat16)
-    grad_imag = (sine * resid_real + cosine * resid_imag).astype(jnp.bfloat16)
-    back = wt_ref[...]
-    grad_ref[0, 0] = jnp.dot(back, grad_real, preferred_element_type=f32)
-    grad_ref[1, 0] = jnp.dot(back, grad_imag, preferred_element_type=f32)
-
-
-def local_step(scale, weights, pick, cosine, sine, ctf, phase, full_map, images):
+    _, groups, depth, cols = map_ref.shape
+    rounds = groups // 2
+    chips = groups
+    tiles, planes = out_ref.shape[1], depth // out_ref.shape[1]
+    part = out_ref.shape[2]
+    me = lax.axis_index("bins")
+    chip, core = me // 2, me % 2
+    band = lax.axis_index("shells")
+    tile = min(256, cols)
+    mesh_ids = pl.DeviceIdType.MESH
+
+    partner = {"bins": chip * 2 + (1 - core)}
+    peers = [{"bins": (chip + r) % chips * 2 + core} for r in range(1, chips)]
+    stack = [{"shells": (band + q) % bands} for q in range(1, bands)]
+    barrier = pltpu.get_barrier_semaphore()
+    for other in [partner] + peers + stack:
+        pl.semaphore_signal(barrier, inc=1, device_id=other, device_id_type=mesh_ids)
+    pl.semaphore_wait(barrier, 1 + len(peers) + len(stack))
+    loss_ref[...] = jnp.zeros_like(loss_ref)
+
+    def compute(group, target):
+        def columns(at, carry):
+            inside = pl.ds(pl.multiple_of(at * tile, tile), tile)
+            base = group * cols + at * tile
+            cells = pl.ds(pl.multiple_of(base, tile), tile)
+            imag_cells = pl.ds(pl.multiple_of(groups * cols + base, tile), tile)
+            weights = w_ref[...]
+            phases = phase_ref[:, cells]
+            part_a = jnp.dot(weights, map_ref[0, group, :, inside], preferred_element_type=f32)
+            part_b = jnp.dot(weights, map_ref[1, group, :, inside], preferred_element_type=f32)
+            contrast = jnp.dot(pick_ref[...], ctf_ref[:, cells], preferred_element_type=f32)
+            cosine = contrast * jnp.dot(cos_ref[...], phases, preferred_element_type=f32)
+            sine = contrast * jnp.dot(sin_ref[...], phases, preferred_element_type=f32)
+            resid_real = cosine * part_a + sine * part_b - img_ref[:, cells].astype(f32)
+            resid_imag = cosine * part_b - sine * part_a - img_ref[:, imag_cells].astype(f32)
+            square = resid_real * resid_real + resid_imag * resid_imag
+            total = square[:, :128]
+            for lane in range(128, tile, 128):
+                total = total + square[:, lane : lane + 128]
+            loss_ref[...] += total
+            cosine = scale * cosine
+            sine = scale * sine
+            grad_real = (cosine * resid_real - sine * resid_imag).astype(jnp.bfloat16)
+            grad_imag = (sine * resid_real + cosine * resid_imag).astype(jnp.bfloat16)
+            back = wt_ref[...]
+            target[0, :, inside] = jnp.dot(back, grad_real, preferred_element_type=f32)
+            target[1, :, inside] = jnp.dot(back, grad_imag, preferred_element_type=f32)
+            return carry
+
+        lax.fori_loop(0, cols // tile, columns, 0)
+
+    def to_partner(turn):
+        return pltpu.make_async_remote_copy(
+            src_ref=theirs.at[turn], dst_ref=pair_in.at[turn],
+            send_sem=pair_send.at[turn], recv_sem=pair_recv.at[turn],
+            device_id=partner, device_id_type=mesh_ids,
+        )
+
+    def rows_of(t):
+        return pl.ds(t * planes, planes)
+
+    def to_chip(turn, hop, t):
+        half = (chip + hop) % chips // rounds
+        return pltpu.make_async_remote_copy(
+            src_ref=mine.at[turn, half, rows_of(t)], dst_ref=chip_in.at[hop - 1, rows_of(t)],
+            send_sem=chip_send.at[hop - 1, t], recv_sem=chip_recv.at[hop - 1, t],
+            device_id=peers[hop - 1], device_id_type=mesh_ids,
+        )
+
+    def to_band(hop, t):
+        there = (band + hop) % bands
+        return pltpu.make_async_remote_copy(
+            src_ref=final.at[pl.ds(pl.multiple_of(t * planes + there * part, 8), part)],
+            dst_ref=out_ref.at[band, t],
+            send_sem=band_send.at[hop - 1, t], recv_sem=band_recv.at[hop - 1, t],
+            device_id=stack[hop - 1], device_id_type=mesh_ids,
+        )
+
+    for turn in range(rounds):
+        pair = (chip + turn + 1) % rounds
+        compute(pair * 2 + (1 - core), theirs.at[turn])
+        to_partner(turn).start()
+        compute(pair * 2 + core, mine.at[turn])
+        to_partner(turn).wait_recv()
+        hops = [(turn + 1) % chips, (turn + 1 + rounds) % chips]
+        for t in range(tiles):
+            for half in range(2):
+                mine[turn, half, rows_of(t)] += pair_in[turn, half, rows_of(t)]
+            for hop in hops:
+                if hop:
+                    to_chip(turn, hop, t).start()
+
+    own = chip // rounds
+    for t in range(tiles):
+        total = mine[rounds - 1, own, rows_of(t)]
+        for hop in range(1, chips):
+            to_chip((hop - 1) % rounds, hop, t).wait_recv()
+            total = total + chip_in[hop - 1, rows_of(t)]
+        final[rows_of(t)] = total
+        for hop in range(1, bands):
+            to_band(hop, t).start()
+        out_ref[band, t] = final[pl.ds(pl.multiple_of(t * planes + band * part, 8), part)]
+
+    for turn in range(rounds):
+        to_partner(turn).wait_send()
+    for t in range(tiles):
+        for hop in range(1, chips):
+            to_chip((hop - 1) % rounds, hop, t).wait_send()
+        for hop in range(1, bands):
+            to_band(hop, t).wait()
+
+
+def local_step(scale, bands, tiles, weights, pick, cosine, sine, ctf, phase, full_map, images):
     rows, depth = weights.shape
-    halves, groups, _, cols = full_map.shape
-    tile = min(256, cols)
-    steps = groups * cols // tile
-    per = cols // tile
-
-    def whole(a):
-        return pl.BlockSpec(a.shape, lambda g: (0,) * a.ndim)
-
-    back = weights.T
-    split = pl.BlockSpec((halves, 1, depth, tile), lambda g: (0, g // per, 0, g % per))
+    _, groups, _, cols = full_map.shape
+    rounds, part = groups // 2, depth // tiles // bands
+    f32 = jnp.float32
+    vmem = pl.BlockSpec(memory_space=pltpu.VMEM)
+    dma = pltpu.SemaphoreType.DMA
     return pl.pallas_call(
-        lambda *refs: step_body(scale, *refs),
-        grid=(steps,),
-        in_specs=[
-            whole(weights), whole(back), whole(pick), whole(cosine), whole(sine),
-            pl.BlockSpec((ctf.shape[0], tile), lambda g: (0, g)),
-            pl.BlockSpec((phase.shape[0], tile), lambda g: (0, g)),
-            split,
-            pl.BlockSpec((rows, tile), lambda g: (0, g)),
-            pl.BlockSpec((rows, tile), lambda g: (0, steps + g)),
+        lambda *refs: fused_step(scale, bands, *refs),
+        in_specs=[vmem] * 9,
+        out_specs=[vmem] * 2,
+        out_shape=[
+            jax.ShapeDtypeStruct((bands, tiles, part, cols), f32),
+            jax.ShapeDtypeStruct((rows, 128), f32),
         ],
-        out_specs=[split, pl.BlockSpec((rows, 128), lambda g: (0, 0))],
-        out_shape=[
-            jax.ShapeDtypeStruct(full_map.shape, jnp.float32),
-            jax.ShapeDtypeStruct((rows, 128), jnp.float32),
+        scratch_shapes=[
+            pltpu.VMEM((rounds, 2, depth, cols), f32),
+            pltpu.VMEM((rounds, 2, depth, cols), f32),
+            pltpu.VMEM((rounds, 2, depth, cols), f32),
+            pltpu.VMEM((groups - 1, depth, cols), f32),
+            pltpu.VMEM((depth, cols), f32),
+            dma((rounds,)),
+            dma((rounds,)),
+            dma((groups - 1, tiles)),
+            dma((groups - 1, tiles)),
+            dma((bands - 1, tiles)),
+            dma((bands - 1, tiles)),
         ],
-        compiler_params=pltpu.CompilerParams(vmem_limit_bytes=48 * 2**20),
-    )(weights, back, pick, cosine, sine, ctf, phase, full_map, images, images)
+        compiler_params=pltpu.CompilerParams(
+            vmem_limit_bytes=62 * 2**20, collective_id=0, has_side_effects=True
+        ),
+    )(weights, weights.T, pick, cosine, sine, ctf, phase, full_map, images)
 
 
 def on_device(map_tiles, images, pose_bin, rot_index, shift_index, defocus_class, tile_slots):
@@ -182,8 +275,8 @@
     pick, cosine, sine = selectors(per_row(shift_index), per_row(defocus_class), tile_safe, pad)
     ctf = contrast_table(band_value, plane_count, band_count)
     phase = phase_table(plane_count, pad)
-    partial, losses = local_step(
-        grad_scale, weights, pick, cosine, sine, ctf, phase,
+    gradient, losses = local_step(
+        grad_scale, band_count, tile_count, weights, pick, cosine, sine, ctf, phase,
         gathered.reshape(2, bin_count // 2, depth, shard_cols),
         images.reshape(rows, column_count),
     )
@@ -191,16 +284,6 @@
         2.0
         * jnp.sum((losses * occupied[:, None]).reshape(part_count, slot_count * 128), axis=1)
         / (slot_count * column_count)
-    )
-    grad_shard = lax.psum_scatter(
-        partial.reshape(bin_count, depth, shard_cols), "bins", scatter_dimension=0, tiled=True
-    )
-    gradient = lax.all_to_all(
-        grad_shard.reshape(1, tile_count, plane_count, shard_cols),
-        "shells",
-        split_axis=2,
-        concat_axis=0,
-        tiled=True,
     )
     return (gradient, band_loss[:, None])
 

time: 193 us -> 138 us (0.72)
  waiting for transfers between devices: 99.5 us -> 9.73 us
  Pallas kernels: 20.8 us -> 75.2 us
  local copies, waits for them, and re-layouts: 34.8 us -> 18.2 us
  starting transfers between devices: 4.67 us -> 0.04 us
    reduce_scatter x1 -> x0, waiting for transfers between devices: 74.3 us -> none  [on_device(): lax.psum_scatter(partial.reshape(bin_count, depth, shard_cols), 'bins', s...]
    pallas_call x1, Pallas kernels: 20.8 us -> 75.2 us  [local_step(): pl.pallas_call(lambda *refs: fused_step(scale, bands, *refs), in_specs=[v...]
    all_to_all x1 -> x0, waiting for transfers between devices: 24.5 us -> none  [on_device(): lax.all_to_all(grad_shard.reshape(1, tile_count, plane_count, shard_cols)...]
    concatenate x1, local copies, waits for them, and re-layouts: 10.3 us -> 0.7 us  [phase_table(): return jnp.concatenate(both, axis=0)]
    all_gather x1, waiting for transfers between devices: 0.02 us -> 9.05 us  [on_device(): lax.all_gather(map_tiles.reshape(1, depth, shard_cols), 'bins', axis=0, t...]
    convert_element_type x1 -> x0, other arithmetic: 4.96 us -> none  [split_halves(): low = (table - rounded).astype(jnp.bfloat16)]
    all_to_all x1 -> x0, starting transfers between devices: 4.6 us -> none  [on_device(): lax.all_to_all(grad_shard.reshape(1, tile_count, plane_count, shard_cols)...]
    unnamed x0 -> x4, other arithmetic: none -> 3.72 us
  transfers between devices with their start and end apart: 3 -> 1, of which waited for: 2 -> 1; matrix products, arithmetic and copies ran while one was open for 23% -> 24% of each run, Pallas kernels for 0% -> 0%
where the time goes in v2:
time: 138 us; the launch traced here: 136 us
  Pallas kernels  75.2 us (54%)
  local copies, waits for them, and re-layouts  18.2 us (13%)
  other arithmetic  18.2 us (13%)
  between operations  14.2 us (10%)
  waiting for transfers between devices  9.73 us (7%)
    pallas_call x1, Pallas kernels, local_step(): pl.pallas_call(lambda *refs: fused_step(scale, bands, *refs), in_specs=[v...  75.2 us
    reshape x1, local copies, waits for them, and re-layouts, on_device(): images.reshape(rows, column_count)  13.3 us
    all_gather x1, waiting for transfers between devices, on_device(): lax.all_gather(map_tiles.reshape(1, depth, shard_cols), 'bins', axis=0, t...  9.05 us
    convert_element_type x1, other arithmetic, split_halves(): high = rounded.astype(jnp.bfloat16)  4.33 us
    unnamed x4, other arithmetic  3.72 us
  transfers between devices with their start and end apart: 1, of which 1 were waited for; matrix products, arithmetic and copies ran while one was open for 24% of the time, Pallas kernels for 0%

profile of v2, /device:TPU:0, one launch (start us, length us, event | category | flops | bytes accessed | tf_op | source)
XLA Modules:
  0.0 135.6 jit_solution(6030702857838551528)
XLA Ops:
  7.2 0.7 all-gather.2.cloned.1.call-update
  8.0 0.7 convert_multiply_fusion.2
  8.7 0.7 broadcast_multiply_fusion.2
  9.4 0.7 broadcast_multiply_fusion.1
  10.3 0.1 broadcast_in_dim.43
  10.4 0.1 mul.345
  10.5 0.7 multiply_add_fusion.2
  11.2 0.1 broadcast_in_dim.47
  11.3 0.1 add.369
  11.5 0.1 mul.363
  11.7 0.8 broadcast_in_dim.51
  12.5 0.1 reshape.449
  12.6 0.5 fusion.19
  13.2 0.5 fusion.18
  13.7 13.3 %reshape.452.refs_8_ = bf16[512,8192]{1,0:T(8,128)(2,1)} reshape(bf16[256,1,2,8192]{3,2,1,0:T(2,128)(2,1)} %param.8) | data formatting | bytes 16777216 | tf_op jit(solution)/shard_map/reshape | solution.py:281
  27.2 0.8 compare_convert_fusion.refs_2_
  28.0 1.0 fusion.12.refs_1_
  28.9 1.4 %fusion.4 = (bf16[512,256]{1,0:T(8,128)(2,1)}, bf16[512,256]{1,0:T(8,128)(2,1)}, bf16[512,256]{1,0:T(8,128)(2,1)}) fusion(f32[256]{0:T(256)S(1)} %and_convert_fusion, f32[512]{0:T(512)S(1)} %select_select_fusion, f32[256]{0:T(256)S(1)} %compare_convert_fusion.1, f32[512]{0:T(512)S(1)} %get-tuple-element.14, s32[256]{0:T(256)S(1)} %and_select_fusion.4, ...), kind=kLoop, calls=%fused_computation.20 | loop fusion | flops 2490368 | bytes 802304 | tf_op jit(solution)/shard_map/convert_element_type | solution.py:76
  30.4 0.9 fusion.15
  31.3 1.0 fusion.14
  32.2 0.9 fusion.16
  33.1 0.9 fusion.13
  34.1 0.7 broadcast_dynamic-update-slice_fusion.refs_6_
  34.8 4.3 %reduce-precision_convert_fusion = (bf16[64,4096]{1,0:T(8,128)(2,1)S(1)}, bf16[64,4096]{1,0:T(8,128)(2,1)S(1)}) fusion(f32[]{:T(128)S(6)} %div.111, s32[4096]{0:T(1024)S(1)} %get-tuple-element.30, s32[64]{0:T(128)S(1)} %get-tuple-element.33, s32[4096]{0:T(1024)S(1)} %get-tuple-element.31, s32[64]{0:T(128)S(1)} %get-tuple-element.32, f32[64]{0:T(128)S(1)} %fusion.46), kind=kLoop, calls=%fused_computation.1 | loop fusion | flops 4718592 | bytes 1082116 | tf_op jit(solution)/shard_map/convert_element_type | solution.py:19
  39.1 1.1 pad_maximum_fusion.refs_5_
  40.2 9.0 %all-gather.2.cloned.1.call-done = bf16[8,256,1024]{2,1,0:T(8,128)(2,1)} async-done(((bf16[1,256,1024]{2,1,0:T(8,128)(2,1)}), bf16[8,256,1024]{2,1,0:T(8,128)(2,1)}) %all-gather.2.cloned.1.call-update) | async-done | bytes 4194320 | tf_op jit(solution)/shard_map/all_gather | solution.py:258
  49.2 75.2 %shard_map.86 = (f32[4,4,16,1024]{3,2,1,0:T(8,128)}, f32[512,128]{1,0:T(8,128)}) custom-call(bf16[512,256]{1,0:T(8,128)(2,1)} %get-tuple-element.29.refs_0_, bf16[256,512]{1,0:T(8,128)(2,1)} %fusion.12.refs_1_, bf16[512,128]{1,0:T(8,128)(2,1)} %compare_convert_fusion.refs_2_, bf16[512,256]{1,0:T(8,128)(2,1)} %get-tuple-element.23.refs_3_, ...), custom_call_target="tpu_custom_call" | custom-call | tf_op jit(solution)/shard_map/pallas_call | solution.py:221
  124.4 1.2 multiply_reduce_fusion
  125.6 0.1 reduce_sum.27
  125.8 0.1 reduce_sum.28
  125.9 0.6 broadcast_multiply_fusion
  126.5 2.3 %copy.18 = f32[4,4,16,1024]{3,2,1,0:T(8,128)} copy(f32[4,4,16,1024]{3,2,1,0:T(8,128)} %get-tuple-element.36) | data formatting | bytes 2097152
  (24 shorter events, 0.5 us)
Async XLA Ops:
  7.2 2.9 %copy-start = (s32[8,4,2]{0,2,1:T(2,128)S(1)}, s32[8,4,2]{0,2,1:T(2,128)}, u32[]{:S(2)}) copy-start(s32[8,4,2]{0,2,1:T(2,128)} %param.13) | copy-start | bytes 772
  7.2 42.0 %all-gather.2.cloned.1.call-start = ((), (), s32[]{:S(2)}) async-start(), calls=%async_computation | async-start | bytes 4718592 | tf_op jit(solution)/shard_map/all_gather | solution.py:258
Sparse Core Ops, SparseCore 0:
  9.9 39.3 all-gather.1

commit v3 on v2

--- a/solution.py
+++ b/solution.py
@@ -93,9 +93,10 @@
 
 
 def fused_step(
-    scale, bands, w_ref, wt_ref, pick_ref, cos_ref, sin_ref, ctf_ref, phase_ref, map_ref, img_ref,
+    scale, bands, w_ref, wt_ref, pick_ref, cos_ref, sin_ref, ctf_ref, phase_ref, shard_ref, img_ref,
     out_ref, loss_ref,
-    mine, theirs, pair_in, chip_in, final,
+    map_ref, mine, theirs, pair_in, chip_in, final,
+    own_sem, map_send, map_recv, share_send, share_recv,
     pair_send, pair_recv, chip_send, chip_recv, band_send, band_recv,
 ):
     f32 = jnp.float32
@@ -117,14 +118,46 @@
     for other in [partner] + peers + stack:
         pl.semaphore_signal(barrier, inc=1, device_id=other, device_id_type=mesh_ids)
     pl.semaphore_wait(barrier, 1 + len(peers) + len(stack))
+
+    def block_of(device):
+        return map_ref.at[device // groups, device % groups]
+
+    def to_map(hop):
+        return pltpu.make_async_remote_copy(
+            src_ref=shard_ref, dst_ref=block_of(me),
+            send_sem=map_send.at[hop - 1], recv_sem=map_recv.at[hop - 1],
+            device_id=peers[hop - 1], device_id_type=mesh_ids,
+        )
+
+    def to_share(hop):
+        source = (chip - hop + chips) % chips * 2 + core
+        return pltpu.make_async_remote_copy(
+            src_ref=block_of(source) if hop else shard_ref, dst_ref=block_of(source),
+            send_sem=share_send.at[hop], recv_sem=share_recv.at[hop],
+            device_id=partner, device_id_type=mesh_ids,
+        )
+
+    def hops_of(turn):
+        return [(turn + 1) % chips, (turn + 1 + rounds) % chips]
+
+    for turn in range(rounds):
+        for hop in hops_of(turn):
+            if hop:
+                to_map(hop).start()
+    to_share(0).start()
+    keep = pltpu.make_async_copy(shard_ref, block_of(me), own_sem)
+    keep.start()
     loss_ref[...] = jnp.zeros_like(loss_ref)
+
+    def observed(start):
+        lanes = [img_ref[start // 128 + at].astype(f32) for at in range(tile // 128)]
+        return jnp.concatenate(lanes, axis=1)
 
     def compute(group, target):
         def columns(at, carry):
             inside = pl.ds(pl.multiple_of(at * tile, tile), tile)
             base = group * cols + at * tile
             cells = pl.ds(pl.multiple_of(base, tile), tile)
-            imag_cells = pl.ds(pl.multiple_of(groups * cols + base, tile), tile)
             weights = w_ref[...]
             phases = phase_ref[:, cells]
             part_a = jnp.dot(weights, map_ref[0, group, :, inside], preferred_element_type=f32)
@@ -132,8 +165,8 @@
             contrast = jnp.dot(pick_ref[...], ctf_ref[:, cells], preferred_element_type=f32)
             cosine = contrast * jnp.dot(cos_ref[...], phases, preferred_element_type=f32)
             sine = contrast * jnp.dot(sin_ref[...], phases, preferred_element_type=f32)
-            resid_real = cosine * part_a + sine * part_b - img_ref[:, cells].astype(f32)
-            resid_imag = cosine * part_b - sine * part_a - img_ref[:, imag_cells].astype(f32)
+            resid_real = cosine * part_a + sine * part_b - observed(base)
+            resid_imag = cosine * part_b - sine * part_a - observed(groups * cols + base)
             square = resid_real * resid_real + resid_imag * resid_imag
             total = square[:, :128]
             for lane in range(128, tile, 128):
@@ -177,19 +210,31 @@
             device_id=stack[hop - 1], device_id_type=mesh_ids,
         )
 
-    for turn in range(rounds):
-        pair = (chip + turn + 1) % rounds
-        compute(pair * 2 + (1 - core), theirs.at[turn])
-        to_partner(turn).start()
-        compute(pair * 2 + core, mine.at[turn])
+    def combine(turn):
         to_partner(turn).wait_recv()
-        hops = [(turn + 1) % chips, (turn + 1 + rounds) % chips]
         for t in range(tiles):
             for half in range(2):
                 mine[turn, half, rows_of(t)] += pair_in[turn, half, rows_of(t)]
-            for hop in hops:
+            for hop in hops_of(turn):
                 if hop:
                     to_chip(turn, hop, t).start()
+
+    for turn in range(rounds):
+        pair = (chip + turn + 1) % rounds
+        for hop in hops_of(turn):
+            if hop:
+                to_map(chips - hop).wait_recv()
+                to_share(chips - hop).start()
+            else:
+                keep.wait()
+        compute(pair * 2 + core, mine.at[turn])
+        if turn:
+            combine(turn - 1)
+        for hop in hops_of(turn):
+            to_share((chips - hop) % chips).wait_recv()
+        compute(pair * 2 + (1 - core), theirs.at[turn])
+        to_partner(turn).start()
+    combine(rounds - 1)
 
     own = chip // rounds
     for t in range(tiles):
@@ -202,6 +247,10 @@
             to_band(hop, t).start()
         out_ref[band, t] = final[pl.ds(pl.multiple_of(t * planes + band * part, 8), part)]
 
+    to_share(0).wait_send()
+    for hop in range(1, chips):
+        to_map(hop).wait_send()
+        to_share(hop).wait_send()
     for turn in range(rounds):
         to_partner(turn).wait_send()
     for t in range(tiles):
@@ -211,9 +260,9 @@
             to_band(hop, t).wait()
 
 
-def local_step(scale, bands, tiles, weights, pick, cosine, sine, ctf, phase, full_map, images):
+def local_step(scale, bands, tiles, weights, pick, cosine, sine, ctf, phase, shard, bins, images):
     rows, depth = weights.shape
-    _, groups, _, cols = full_map.shape
+    groups, cols = bins // 2, shard.shape[1]
     rounds, part = groups // 2, depth // tiles // bands
     f32 = jnp.float32
     vmem = pl.BlockSpec(memory_space=pltpu.VMEM)
@@ -227,11 +276,17 @@
             jax.ShapeDtypeStruct((rows, 128), f32),
         ],
         scratch_shapes=[
+            pltpu.VMEM((2, groups, depth, cols), jnp.bfloat16),
             pltpu.VMEM((rounds, 2, depth, cols), f32),
             pltpu.VMEM((rounds, 2, depth, cols), f32),
             pltpu.VMEM((rounds, 2, depth, cols), f32),
             pltpu.VMEM((groups - 1, depth, cols), f32),
             pltpu.VMEM((depth, cols), f32),
+            dma,
+            dma((groups - 1,)),
+            dma((groups - 1,)),
+            dma((groups,)),
+            dma((groups,)),
             dma((rounds,)),
             dma((rounds,)),
             dma((groups - 1, tiles)),
@@ -242,7 +297,7 @@
         compiler_params=pltpu.CompilerParams(
             vmem_limit_bytes=62 * 2**20, collective_id=0, has_side_effects=True
         ),
-    )(weights, weights.T, pick, cosine, sine, ctf, phase, full_map, images)
+    )(weights, weights.T, pick, cosine, sine, ctf, phase, shard, images)
 
 
 def on_device(map_tiles, images, pose_bin, rot_index, shift_index, defocus_class, tile_slots):
@@ -255,7 +310,11 @@
     rows = part_count * slot_count
     depth = tile_count * plane_count
     grad_scale = NOISE_PRECISION / math.sqrt(part_count * bin_count)
-    gathered = lax.all_gather(map_tiles.reshape(1, depth, shard_cols), "bins", axis=0, tiled=True)
+    lane_images = (
+        images.reshape(part_count, slot_count, column_count // 128, 128)
+        .transpose(2, 0, 1, 3)
+        .reshape(column_count // 128, rows, 128)
+    )
     band_slots = lax.dynamic_index_in_dim(tile_slots, band_index, 1, keepdims=False)
 
     def per_row(values):
@@ -277,8 +336,7 @@
     phase = phase_table(plane_count, pad)
     gradient, losses = local_step(
         grad_scale, band_count, tile_count, weights, pick, cosine, sine, ctf, phase,
-        gathered.reshape(2, bin_count // 2, depth, shard_cols),
-        images.reshape(rows, column_count),
+        map_tiles.reshape(depth, shard_cols), bin_count, lane_images,
     )
     band_loss = (
         2.0

time: 138 us -> 159 us (1.15)
  Pallas kernels: 75.2 us -> 105 us
  local copies, waits for them, and re-layouts: 18.2 us -> 33.4 us
  between operations: 14.2 us -> 0.81 us
  waiting for transfers between devices: 9.73 us -> 0 us
    pallas_call x1, Pallas kernels: 75.2 us -> 105 us  [local_step(): pl.pallas_call(lambda *refs: fused_step(scale, bands, *refs), in_specs=[v...]
    reshape x1 -> x2, local copies, waits for them, and re-layouts: 13.3 us -> 27.8 us  [on_device(): images.reshape(part_count, slot_count, column_count // 128, 128)]
    all_gather x1 -> x0, waiting for transfers between devices: 9.05 us -> none  [on_device(): lax.all_gather(map_tiles.reshape(1, depth, shard_cols), 'bins', axis=0, t...]
  transfers between devices with their start and end apart: 1 -> 0, of which waited for: 1 -> 0; matrix products, arithmetic and copies ran while one was open for 24% -> 0% of each run, Pallas kernels for 0% -> 0%
where the time goes in v3:
time: 159 us; the launch traced here: 157 us
  Pallas kernels  105 us (66%)
  local copies, waits for them, and re-layouts  33.4 us (21%)
  other arithmetic  18.3 us (12%)
    pallas_call x1, Pallas kernels, local_step(): pl.pallas_call(lambda *refs: fused_step(scale, bands, *refs), in_specs=[v...  105 us
    reshape x2, local copies, waits for them, and re-layouts, on_device(): images.reshape(part_count, slot_count, column_count // 128, 128)  27.8 us
    convert_element_type x1, other arithmetic, split_halves(): high = rounded.astype(jnp.bfloat16)  4.33 us
    unnamed x4, other arithmetic  3.68 us

profile of v3, /device:TPU:0, one launch (start us, length us, event | category | flops | bytes accessed | tf_op | source)
XLA Modules:
  0.0 157.1 jit_solution(11742163989637843487)
XLA Ops:
  0.7 0.7 copy-done
  1.4 0.7 broadcast_multiply_fusion.1
  2.0 0.7 convert_multiply_fusion.2
  2.7 0.7 multiply_add_fusion.2
  3.4 0.7 broadcast_multiply_fusion.2
  4.3 0.1 broadcast_in_dim.43
  4.4 0.1 mul.345
  4.8 0.1 add.369
  4.9 0.1 broadcast_in_dim.50
  5.0 0.1 mul.363
  5.2 0.8 compare_convert_fusion.refs_2_
  6.0 0.8 broadcast_in_dim.51
  6.7 0.1 reshape.449
  7.0 1.0 fusion.12.refs_1_
  8.0 0.5 fusion.18
  8.5 0.5 fusion.19
  9.1 1.5 fusion.4
  10.5 4.3 %reduce-precision_convert_fusion = (bf16[64,4096]{1,0:T(8,128)(2,1)S(1)}, bf16[64,4096]{1,0:T(8,128)(2,1)S(1)}) fusion(f32[]{:T(128)S(6)} %div.111, s32[4096]{0:T(1024)S(1)} %get-tuple-element.30, s32[64]{0:T(128)S(1)} %get-tuple-element.33, s32[4096]{0:T(1024)S(1)} %get-tuple-element.31, s32[64]{0:T(128)S(1)} %get-tuple-element.32, f32[64]{0:T(128)S(1)} %fusion.46), kind=kLoop, calls=%fused_computation.1 | loop fusion | flops 4718592 | bytes 1082116 | tf_op jit(solution)/shard_map/convert_element_type | solution.py:19
  14.9 1.1 pad_maximum_fusion.refs_5_
  15.9 0.9 fusion.15
  16.8 0.9 fusion.14
  17.8 0.9 fusion.16
  18.6 1.0 fusion.13
  19.6 0.7 broadcast_dynamic-update-slice_fusion.refs_6_
  20.3 14.6 %reshape.451 = bf16[256,2,64,128]{3,2,1,0:T(8,128)(2,1)} reshape(bf16[256,1,2,8192]{3,2,1,0:T(2,128)(2,1)} %param.8) | data formatting | bytes 16777216 | tf_op jit(solution)/shard_map/reshape | solution.py:314
  34.9 13.2 %copy.14 = bf16[256,2,64,128]{3,1,0,2:T(2,128)(2,1)} copy(bf16[256,2,64,128]{3,2,1,0:T(8,128)(2,1)} %reshape.451) | data formatting | bytes 16777216 | tf_op jit(solution)/shard_map/reshape | solution.py:314
  48.1 104.7 %shard_map.86 = (f32[4,4,16,1024]{3,2,1,0:T(8,128)}, f32[512,128]{1,0:T(8,128)}) custom-call(bf16[512,256]{1,0:T(8,128)(2,1)} %get-tuple-element.29.refs_0_, bf16[256,512]{1,0:T(8,128)(2,1)} %fusion.12.refs_1_, bf16[512,128]{1,0:T(8,128)(2,1)} %compare_convert_fusion.refs_2_, bf16[512,256]{1,0:T(8,128)(2,1)} %get-tuple-element.23.refs_3_, ...), custom_call_target="tpu_custom_call" | custom-call | tf_op jit(solution)/shard_map/pallas_call | solution.py:270
  152.8 1.2 multiply_reduce_fusion
  154.0 0.1 reduce_sum.27
  154.1 0.1 reduce_sum.28
  154.2 0.6 broadcast_multiply_fusion
  154.8 2.3 %copy.20 = f32[4,4,16,1024]{3,2,1,0:T(8,128)} copy(f32[4,4,16,1024]{3,2,1,0:T(8,128)} %get-tuple-element.36) | data formatting | bytes 2097152
  (22 shorter events, 0.5 us)
Async XLA Ops:
  0.6 0.7 copy-start

commit v4 on v3

--- a/solution.py
+++ b/solution.py
@@ -93,10 +93,10 @@
 
 
 def fused_step(
-    scale, bands, w_ref, wt_ref, pick_ref, cos_ref, sin_ref, ctf_ref, phase_ref, shard_ref, img_ref,
+    scale, bands, w_ref, wt_ref, pick_ref, cos_ref, sin_ref, ctf_ref, phase_ref, shard_ref, images_ref,
     out_ref, loss_ref,
     map_ref, mine, theirs, pair_in, chip_in, final,
-    own_sem, map_send, map_recv, share_send, share_recv,
+    img_ref, img_sem, own_sem, map_send, map_recv, share_send, share_recv,
     pair_send, pair_recv, chip_send, chip_recv, band_send, band_recv,
 ):
     f32 = jnp.float32
@@ -111,6 +111,18 @@
     tile = min(256, cols)
     mesh_ids = pl.DeviceIdType.MESH
 
+    rows = w_ref.shape[0]
+
+    def fetch(lane):
+        cells = pl.ds(pl.multiple_of(lane * 128, 128), 128)
+        return pltpu.make_async_copy(
+            images_ref.at[:, 0, :, cells], img_ref.at[lane], img_sem.at[lane]
+        )
+
+    def start_fetch(lane, carry):
+        fetch(lane).start()
+        return carry
+
     partner = {"bins": chip * 2 + (1 - core)}
     peers = [{"bins": (chip + r) % chips * 2 + core} for r in range(1, chips)]
     stack = [{"shells": (band + q) % bands} for q in range(1, bands)]
@@ -147,10 +159,15 @@
     to_share(0).start()
     keep = pltpu.make_async_copy(shard_ref, block_of(me), own_sem)
     keep.start()
+    lax.fori_loop(0, img_ref.shape[0], start_fetch, 0)
     loss_ref[...] = jnp.zeros_like(loss_ref)
 
     def observed(start):
-        lanes = [img_ref[start // 128 + at].astype(f32) for at in range(tile // 128)]
+        lanes = []
+        for at in range(tile // 128):
+            lane = start // 128 + at
+            fetch(lane).wait()
+            lanes.append(img_ref[lane].reshape(rows, 128).astype(f32))
         return jnp.concatenate(lanes, axis=1)
 
     def compute(group, target):
@@ -265,11 +282,12 @@
     groups, cols = bins // 2, shard.shape[1]
     rounds, part = groups // 2, depth // tiles // bands
     f32 = jnp.float32
+    lanes = images.shape[3] // 128
     vmem = pl.BlockSpec(memory_space=pltpu.VMEM)
     dma = pltpu.SemaphoreType.DMA
     return pl.pallas_call(
         lambda *refs: fused_step(scale, bands, *refs),
-        in_specs=[vmem] * 9,
+        in_specs=[vmem] * 8 + [pl.BlockSpec(memory_space=pl.ANY)],
         out_specs=[vmem] * 2,
         out_shape=[
             jax.ShapeDtypeStruct((bands, tiles, part, cols), f32),
@@ -282,6 +300,8 @@
             pltpu.VMEM((rounds, 2, depth, cols), f32),
             pltpu.VMEM((groups - 1, depth, cols), f32),
             pltpu.VMEM((depth, cols), f32),
+            pltpu.VMEM((lanes, images.shape[0], images.shape[2], 128), jnp.bfloat16),
+            dma((lanes,)),
             dma,
             dma((groups - 1,)),
             dma((groups - 1,)),
@@ -310,11 +330,6 @@
     rows = part_count * slot_count
     depth = tile_count * plane_count
     grad_scale = NOISE_PRECISION / math.sqrt(part_count * bin_count)
-    lane_images = (
-        images.reshape(part_count, slot_count, column_count // 128, 128)
-        .transpose(2, 0, 1, 3)
-        .reshape(column_count // 128, rows, 128)
-    )
     band_slots = lax.dynamic_index_in_dim(tile_slots, band_index, 1, keepdims=False)
 
     def per_row(values):
@@ -336,7 +351,7 @@
     phase = phase_table(plane_count, pad)
     gradient, losses = local_step(
         grad_scale, band_count, tile_count, weights, pick, cosine, sine, ctf, phase,
-        map_tiles.reshape(depth, shard_cols), bin_count, lane_images,
+        map_tiles.reshape(depth, shard_cols), bin_count, images,
     )
     band_loss = (
         2.0

time: 159 us -> 131 us (0.82); the launches traced: 157 us -> 131 us
  local copies, waits for them, and re-layouts: 33.4 us -> 4.3 us
  Pallas kernels: 105 us -> 110 us
  other arithmetic: 18.3 us -> 15.7 us
    reshape x2 -> x0, local copies, waits for them, and re-layouts: 27.8 us -> none  [on_device(): images.reshape(part_count, slot_count, column_count // 128, 128)]
    pallas_call x1, Pallas kernels: 105 us -> 110 us  [local_step(): pl.pallas_call(lambda *refs: fused_step(scale, bands, *refs), in_specs=[v...]
where the time goes in v4:
time: 131 us
  Pallas kernels  110 us (84%)
  other arithmetic  15.7 us (12%)
  local copies, waits for them, and re-layouts  4.3 us (3%)
    pallas_call x1, Pallas kernels, local_step(): pl.pallas_call(lambda *refs: fused_step(scale, bands, *refs), in_specs=[v...  110 us
    convert_element_type x1, other arithmetic, split_halves(): high = rounded.astype(jnp.bfloat16)  4.35 us
    unnamed x4, other arithmetic  3.66 us

profile of v4, /device:TPU:0, one launch (start us, length us, event | category | flops | bytes accessed | tf_op | source)
XLA Modules:
  0.0 130.8 jit_solution(9393032014571041628)
XLA Ops:
  0.6 0.0 copy-start
  0.7 0.5 fusion.18
  1.2 0.5 fusion.19
  1.8 0.0 copy-start.1
  1.8 0.9 fusion.15
  2.7 0.9 fusion.14
  3.6 0.9 fusion.16
  4.5 0.9 fusion.13
  5.5 0.7 broadcast_dynamic-update-slice_fusion.refs_6_
  6.2 0.1 copy.11
  6.3 0.1 broadcast_in_dim.44
  6.4 0.1 broadcast_in_dim.43
  6.5 0.1 mul.345
  6.6 0.1 select_reduce_fusion
  6.7 0.1 broadcast_in_dim.51
  6.8 0.1 reshape.443
  7.0 0.1 broadcast_in_dim.47
  7.1 0.1 add.369
  7.2 0.1 select_select_fusion.1
  7.3 0.1 broadcast_in_dim.50
  7.4 0.1 mul.363
  7.7 1.6 %fusion.4 = (bf16[512,256]{1,0:T(8,128)(2,1)}, bf16[512,256]{1,0:T(8,128)(2,1)}, bf16[512,256]{1,0:T(8,128)(2,1)}) fusion(f32[256]{0:T(256)S(1)} %and_convert_fusion, f32[512]{0:T(512)S(1)} %select_select_fusion, f32[256]{0:T(256)S(1)} %compare_convert_fusion.1, f32[512]{0:T(512)S(1)} %get-tuple-element.14, s32[256]{0:T(256)S(1)} %and_select_fusion.4, ...), kind=kLoop, calls=%fused_computation.20 | loop fusion | flops 2490368 | bytes 802304 | tf_op jit(solution)/shard_map/convert_element_type | solution.py:76
  9.3 1.0 fusion.12.refs_1_
  10.3 4.4 %reduce-precision_convert_fusion = (bf16[64,4096]{1,0:T(8,128)(2,1)S(1)}, bf16[64,4096]{1,0:T(8,128)(2,1)S(1)}) fusion(f32[]{:T(128)S(6)} %div.111, s32[4096]{0:T(1024)S(1)} %get-tuple-element.30, s32[64]{0:T(128)S(1)} %get-tuple-element.33, s32[4096]{0:T(1024)S(1)} %get-tuple-element.31, s32[64]{0:T(128)S(1)} %get-tuple-element.32, f32[64]{0:T(128)S(1)} %fusion.46), kind=kLoop, calls=%fused_computation.1 | loop fusion | flops 4718592 | bytes 1082116 | tf_op jit(solution)/shard_map/convert_element_type | solution.py:19
  14.7 1.1 pad_maximum_fusion.refs_5_
  15.7 0.8 compare_convert_fusion.refs_2_
  16.5 110.0 %shard_map.86 = (f32[4,4,16,1024]{3,2,1,0:T(8,128)}, f32[512,128]{1,0:T(8,128)}) custom-call(bf16[512,256]{1,0:T(8,128)(2,1)} %get-tuple-element.29.refs_0_, bf16[256,512]{1,0:T(8,128)(2,1)} %fusion.12.refs_1_, bf16[512,128]{1,0:T(8,128)(2,1)} %compare_convert_fusion.refs_2_, bf16[512,256]{1,0:T(8,128)(2,1)} %get-tuple-element.23.refs_3_, ...), custom_call_target="tpu_custom_call" | custom-call | tf_op jit(solution)/shard_map/pallas_call | solution.py:288
  126.5 1.2 multiply_reduce_fusion
  127.7 0.1 reduce_sum.27
  127.9 0.1 reduce_sum.28
  128.0 0.6 broadcast_multiply_fusion
  128.5 2.3 %copy.17 = f32[4,4,16,1024]{3,2,1,0:T(8,128)} copy(f32[4,4,16,1024]{3,2,1,0:T(8,128)} %get-tuple-element.36) | data formatting | bytes 2097152
  (28 shorter events, 0.1 us)
Async XLA Ops:
  0.6 5.5 %copy-start = (s32[8,4,2]{0,2,1:T(2,128)S(1)}, s32[8,4,2]{0,2,1:T(2,128)}, u32[]{:S(2)}) copy-start(s32[8,4,2]{0,2,1:T(2,128)} %param.13) | copy-start | bytes 772
  1.8 4.6 %copy-start.1 = (s32[256,1]{0,1:T(1,128)S(1)}, s32[256,1]{0,1:T(1,128)}, u32[]{:S(2)}) copy-start(s32[256,1]{0,1:T(1,128)} %param.9) | copy-start | bytes 3076
  1.8 4.9 %copy-start.2 = (s32[256]{0:T(256)S(1)}, s32[256]{0:T(256)}, u32[]{:S(2)}) copy-start(s32[256]{0:T(256)} %param.11) | copy-start | bytes 3076
  2.7 4.3 %copy-start.3 = (s32[256]{0:T(256)S(1)}, s32[256]{0:T(256)}, u32[]{:S(2)}) copy-start(s32[256]{0:T(256)} %param.10) | copy-start | bytes 3076
  2.7 4.6 %copy-start.4 = (s32[256]{0:T(256)S(1)}, s32[256]{0:T(256)}, u32[]{:S(2)}) copy-start(s32[256]{0:T(256)} %param.12) | copy-start | bytes 3076
